TPU v7x, 32 devices: a whole 2x2x4 slice. The times are simulated.
32 devices in a mesh: groups: 2 (over x), tile: 16 (over z, y, core).
Axes of the slice: x: 2, y: 2, z: 4, core: 2. Of those that a mesh axis runs over, the one named last changes fastest.
Arguments:
- queries: bfloat16 [2048, 4096], P(('groups', 'tile')), parts along dimension 0, may hold values from -8 to 8
- key_rows: bfloat16 [2048, 4096], P(('groups', 'tile')), parts along dimension 0, may hold values from -8 to 8
- values: bfloat16 [2048, 4096], P(('groups', 'tile')), parts along dimension 0, may hold values from -6 to 6
- modulation: float32 [6, 4096], P('groups'), parts along dimension 0, may hold values from -3 to 3
- expert_in: bfloat16 [4096, 8192], P(None, 'tile'), may hold values from -0.09375 to 0.09375
- expert_out: bfloat16 [8192, 4096], P('tile'), may hold values from -0.125 to 0.125
- routes: int32 [2048, 2], P(('groups', 'tile')), parts along dimension 0, may hold values from 0 to 3, all different within a row; in each aligned block of 64 rows (0 to 63, 64 to 127, ...) at most 48 rows name the same one
- gate_fixed: int32 [2048, 2], P(('groups', 'tile')), parts along dimension 0, may hold values from 64 to 1023
Outputs:
- layer_out: bfloat16 [2048, 4096], P(('groups', 'tile')), parts along dimension 0
There are 2 independent parts, one for each index of `groups`. A program takes and returns all parts, laid end to end along the dimension named above; an argument that names none is the same for every part. Nothing has to cross between parts.
Inputs may be any that keep to these rules, and one draw needn't show every extreme that they name: `routes`: the two experts of a token differ; among the 64 tokens of one tile no expert is named more than 48 times.
All inputs are finite; a program needn't handle non-finite values.
Results may differ from a plain program's by a relative error of at most 0.011.
Values may be sent and summed in bfloat16 or wider, within the bound.
A program may use at most 128 MiB of HBM per device.

v0:
```python
import math

import jax
import jax.numpy as jnp
from jax import lax
from jax.sharding import PartitionSpec as P

HEAD_DIM = 128
D = 4096
SPLIT = 4
TILE_COLS = 8


EPSILON = 1e-06
MASKED = -1e30


def shifted(x, axis, by):
    length = lax.axis_size(axis)
    return lax.ppermute(x, axis, [(i, (i + by) % length) for i in range(length)])


def attend_tile(query_block, banded, allowed):
    rows_here = query_block.shape[0]
    heads_count = D // HEAD_DIM
    query_heads = query_block.reshape(rows_here, heads_count, HEAD_DIM)
    key_heads = banded[0].reshape(banded.shape[1], heads_count, HEAD_DIM)
    value_heads = banded[1].reshape(banded.shape[1], heads_count, HEAD_DIM)
    scores = jnp.einsum(
        "qhd,khd->hqk", query_heads, key_heads, preferred_element_type=jnp.float32
    ) * (1.0 / math.sqrt(HEAD_DIM))
    scores = jnp.where(allowed[None, None, :], scores, MASKED)
    highest = jnp.max(scores, axis=-1, keepdims=True)
    raised = jnp.exp(scores - highest)
    probs = (raised / jnp.sum(raised, axis=-1, keepdims=True)).astype(jnp.bfloat16)
    attended = jnp.einsum("hqk,khd->qhd", probs, value_heads, preferred_element_type=jnp.float32)
    return attended.reshape(rows_here, D).astype(jnp.bfloat16)


def modulate(attended, modulation):
    wide = attended.astype(jnp.float32)
    center = jnp.mean(wide, axis=-1, keepdims=True)
    spread = jnp.mean(jnp.square(wide - center), axis=-1, keepdims=True)
    normed = (wide - center) * lax.rsqrt(spread + EPSILON)
    return (normed * (1.0 + modulation[1]) + modulation[0]).astype(jnp.bfloat16)


def slot_table(flat, experts_count):
    onehot = (flat[:, None] == jnp.arange(experts_count, dtype=jnp.int32)[None, :]).astype(
        jnp.int32
    )
    before = jnp.cumsum(onehot, axis=0) - onehot
    return jnp.sum(before * onehot, axis=1)


def expert_apply(rows, first_weight, second_weight):
    hidden = jax.nn.gelu(
        jnp.dot(rows, first_weight, preferred_element_type=jnp.float32), approximate=True
    ).astype(jnp.bfloat16)
    return jnp.dot(hidden, second_weight, preferred_element_type=jnp.float32).astype(jnp.bfloat16)


def shards(queries, key_rows, values, modulation, expert_in, expert_out, routes, gate_fixed):
    rows_dev = queries.shape[0]
    devices = lax.axis_size("tile")
    position = lax.axis_index("tile")
    grid_rows = devices // TILE_COLS
    tile_number = (position + TILE_COLS // 2) % devices
    grid_row = tile_number // TILE_COLS
    grid_col = tile_number % TILE_COLS
    stacked = jnp.stack([key_rows, values])
    beside_tiles = []
    for offset in (1, -1):
        beside_tiles.append(shifted(stacked, "tile", offset))
    row_strip = jnp.concatenate([beside_tiles[0], stacked, beside_tiles[1]], axis=1)
    levels = []
    for offset in (TILE_COLS, -TILE_COLS):
        levels.append(shifted(row_strip, "tile", offset))
    banded = jnp.concatenate([levels[0], row_strip, levels[1]], axis=1)
    rows_ok = jnp.stack([grid_row > 0, grid_row >= 0, grid_row < grid_rows - 1])
    cols_ok = jnp.stack([grid_col > 0, grid_col >= 0, grid_col < TILE_COLS - 1])
    usable = rows_ok[:, None] & cols_ok[None, :]
    allowed = jnp.broadcast_to(usable[:, :, None], (3, 3, rows_dev)).reshape(9 * rows_dev)
    attended = attend_tile(queries, banded, allowed)
    normed = modulate(attended, modulation)
    experts_count = devices // SPLIT
    capacity = 3 * rows_dev // experts_count
    flat = routes.reshape(-1)
    slots = slot_table(flat, experts_count)
    target = flat * capacity + slots
    chooser = (
        target[None, :] == jnp.arange(experts_count * capacity, dtype=jnp.int32)[:, None]
    ).astype(jnp.bfloat16)
    chooser = chooser.reshape(experts_count * capacity, rows_dev, 2).sum(axis=2)
    buffer = jnp.dot(chooser, normed, preferred_element_type=jnp.float32).astype(jnp.bfloat16)
    copies = jnp.broadcast_to(
        buffer.reshape(experts_count, 1, capacity, D), (experts_count, SPLIT, capacity, D)
    ).reshape(devices, capacity, D)
    received = lax.all_to_all(copies, "tile", split_axis=0, concat_axis=0, tiled=True)
    sources = received.shape[0]
    count = received.shape[1]
    partial_value = expert_apply(received.reshape(sources * count, D), expert_in, expert_out)
    returned = lax.all_to_all(
        partial_value.reshape(sources, count, D), "tile", split_axis=0, concat_axis=0, tiled=True
    )
    summed = jnp.sum(
        returned.reshape(experts_count, SPLIT, capacity, D).astype(jnp.float32), axis=1
    )
    expert_rows = summed.astype(jnp.bfloat16).reshape(experts_count * capacity, D)
    picked = jnp.take(expert_rows, target, axis=0).reshape(rows_dev, 2, D)
    gate_scale = gate_fixed.astype(jnp.float32) / 1024.0
    mixture = jnp.sum(picked.astype(jnp.float32) * gate_scale[:, :, None], axis=1)
    return (attended.astype(jnp.float32) + modulation[2] * mixture).astype(jnp.bfloat16)


def solution(mesh):
    placed = (
        P(("groups", "tile"), None),
        P(("groups", "tile"), None),
        P(("groups", "tile"), None),
        P("groups", None),
        P(None, "tile"),
        P("tile", None),
        P(("groups", "tile"), None),
        P(("groups", "tile"), None),
    )
    return jax.shard_map(
        shards, mesh=mesh, in_specs=placed, out_specs=P(("groups", "tile"), None), check_vma=False
    )
```

profile of v0, /device:TPU:25, one launch (start us, length us, event | category | flops | bytes accessed | tf_op | source)
XLA Modules:
  0.0 503.3 jit_solution(14332862864469286567)
XLA Ops:
  0.0 1.4 pad_maximum_fusion.1
  1.4 1.9 collective-permute-start
  3.2 23.0 %collective-permute-done = bf16[2,64,4096]{2,1,0:T(8,128)(2,1)S(1)} collective-permute-done((bf16[2,64,4096]{2,1,0:T(8,128)(2,1)S(1)}, bf16[2,64,4096]{2,1,0:T(8,128)(2,1)S(1)}, u32[]{:S(2)}, u32[]{:S(2)}) %collective-permute-start) | collective-permute-done | bytes 1048608 | tf_op jit(solution)/shard_map/ppermute | solution.py:20
  26.2 2.0 collective-permute-done.1
  28.2 2.8 pad_maximum_fusion
  32.4 127.7 %collective-permute-done.2 = bf16[2,192,4096]{2,1,0:T(8,128)(2,1)} collective-permute-done((bf16[2,192,4096]{2,1,0:T(8,128)(2,1)}, bf16[2,192,4096]{2,1,0:T(8,128)(2,1)}, u32[]{:S(2)}, u32[]{:S(2)}) %collective-permute-start.2) | collective-permute-done | bytes 3145760 | tf_op jit(solution)/shard_map/ppermute | solution.py:20
  160.2 3.9 constant_dynamic-update-slice_fusion.4
  164.1 1.1 constant_dynamic-update-slice_fusion.3
  165.2 1.1 constant_dynamic-update-slice_fusion.2
  167.3 4.0 constant_dynamic-update-slice_fusion
  171.3 8.7 %slice_bitcast_fusion.1 = (bf16[72,8,32,128]{3,1,2,0:T(8,128)(2,1)}, bf16[72,8,32,128]{3,1,2,0:T(8,128)(2,1)S(1)}) fusion(bf16[2,576,4096]{2,1,0:T(8,128)(2,1)} %constant_dynamic-update-slice_fusion), kind=kLoop, calls=%fused_computation.12 | loop fusion | bytes 18874368
  180.0 3.8 copy.39
  183.8 1.5 copy.40
  185.2 5.0 fusion.5
  190.3 1.8 fusion.55
  192.1 6.0 %convert_reduce_fusion = (f32[64]{0:T(128)S(1)}, bf16[32,128,64]{1,2,0:T(8,128)(2,1)S(1)}) fusion(bf16[576,32,128]{2,1,0:T(8,128)(2,1)S(1)} %bitcast.80, f32[32,64,576]{2,1,0:T(8,128)S(1)} %get-tuple-element.13, f32[32,64]{1,0:T(8,128)S(1)} %get-tuple-element.12), kind=kOutput, calls=%fused_computation.33 | convolution fusion | flops 305135552 | bytes 9969920 | tf_op jit(solution)/shard_map/hqk,khd->qhd/dot_general | solution.py:36
  199.9 142.2 %all_to_all.10 = bf16[16,48,4096]{2,1,0:T(8,128)(2,1)} all-to-all(bf16[16,48,4096]{2,1,0:T(8,128)(2,1)S(1)} %bitcast.75), channel_id=1, replica_groups=mesh['groups'=2,'tile'=16] {'tile'}, dimensions={0} | all-to-all | bytes 12582912 | tf_op jit(solution)/shard_map/all_to_all | solution.py:99
  342.1 13.3 %convolution_convert_fusion = bf16[768,4096]{1,0:T(8,128)(2,1)} fusion(bf16[512,4096]{1,0:T(8,128)(2,1)} %param.13, bf16[768,4096]{1,0:T(8,128)(2,1)} %bitcast.78, bf16[4096,512]{1,0:T(8,128)(2,1)} %param.12), kind=kOutput, calls=%fused_computation.2 | convolution fusion | flops 6449135616 | bytes 20971520 | tf_op jit(solution)/shard_map/dot_general | solution.py:60
  355.3 6.2 %all-to-all-start.1 = ((bf16[16,48,4096]{2,1,0:T(8,128)(2,1)}), bf16[16,48,4096]{2,1,0:T(8,128)(2,1)}, u32[]{:S(2)}, u32[]{:S(2)}) async-start(bf16[16,48,4096]{2,1,0:T(8,128)(2,1)} %bitcast.77), calls=%async_computation.1 | async-start | bytes 12582912 | tf_op jit(solution)/shard_map/all_to_all | solution.py:103
  362.1 128.1 %all-to-all-done.1 = bf16[16,48,4096]{2,1,0:T(8,128)(2,1)} async-done(((bf16[16,48,4096]{2,1,0:T(8,128)(2,1)}), bf16[16,48,4096]{2,1,0:T(8,128)(2,1)}, u32[]{:S(2)}, u32[]{:S(2)}) %all-to-all-start.1) | async-done | bytes 6291488 | tf_op jit(solution)/shard_map/all_to_all | solution.py:103
  490.2 4.1 bitcast_reduce_fusion
  494.3 2.2 gather_fusion
  496.5 1.7 gather.7
  498.2 4.1 multiply_reduce_fusion
  (49 shorter events, 5.7 us)
Async XLA Ops:
  0.0 185.2 %copy-start = (bf16[64,4096]{1,0:T(8,128)(2,1)S(1)}, bf16[64,4096]{1,0:T(8,128)(2,1)}, u32[]{:S(2)}) copy-start(bf16[64,4096]{1,0:T(8,128)(2,1)} %param.8) | copy-start | bytes 1572868
  0.0 31.4 %copy-start.7 = (s32[64,2]{0,1:T(2,128)S(1)}, s32[64,2]{0,1:T(2,128)}, u32[]{:S(2)}) copy-start(s32[64,2]{0,1:T(2,128)} %param.14) | copy-start | bytes 1540
  0.0 32.4 %copy-start.6 = (f32[3,4096]{1,0:T(4,128)S(1)}, f32[3,4096]{1,0:T(4,128)}, u32[]{:S(2)}) copy-start(f32[3,4096]{1,0:T(4,128)} %param.11) | copy-start | bytes 147460
  1.4 24.8 %collective-permute-start = (bf16[2,64,4096]{2,1,0:T(8,128)(2,1)S(1)}, bf16[2,64,4096]{2,1,0:T(8,128)(2,1)S(1)}, u32[]{:S(2)}, u32[]{:S(2)}) collective-permute-start(bf16[2,64,4096]{2,1,0:T(8,128)(2,1)S(1)} %pad_maximum_fusion.1), channel_id=1, source_target_pairs={{0,1},{1,2},{2,3},{3,4},{4,5},{5,6},{6,7},{7,8},{8,9},{9,10},{10,1... | collective-permute-start | bytes 3145736 | tf_op jit(solution)/shard_map/ppermute | solution.py:20
  3.2 24.9 %collective-permute-start.1 = (bf16[2,64,4096]{2,1,0:T(8,128)(2,1)S(1)}, bf16[2,64,4096]{2,1,0:T(8,128)(2,1)S(1)}, u32[]{:S(2)}, u32[]{:S(2)}) collective-permute-start(bf16[2,64,4096]{2,1,0:T(8,128)(2,1)S(1)} %pad_maximum_fusion.1), channel_id=1, source_target_pairs={{0,15},{1,0},{2,1},{3,2},{4,3},{5,4},{6,5},{7,6},{8,7},{9,8},{10,9... | collective-permute-start | bytes 3145736 | tf_op jit(solution)/shard_map/ppermute | solution.py:20
  26.2 2.0 copy-start.4
  31.0 134.2 %copy-start.2 = (bf16[64,4096]{1,0:T(8,128)(2,1)S(1)}, bf16[64,4096]{1,0:T(8,128)(2,1)}, u32[]{:S(2)}) copy-start(bf16[64,4096]{1,0:T(8,128)(2,1)} %param.10) | copy-start | bytes 1572868
  31.0 134.2 %copy-start.3 = (bf16[64,4096]{1,0:T(8,128)(2,1)S(1)}, bf16[64,4096]{1,0:T(8,128)(2,1)}, u32[]{:S(2)}) copy-start(bf16[64,4096]{1,0:T(8,128)(2,1)} %param.9) | copy-start | bytes 1572868
  31.0 129.2 %collective-permute-start.2 = (bf16[2,192,4096]{2,1,0:T(8,128)(2,1)}, bf16[2,192,4096]{2,1,0:T(8,128)(2,1)}, u32[]{:S(2)}, u32[]{:S(2)}) collective-permute-start(bf16[2,192,4096]{2,1,0:T(8,128)(2,1)} %pad_maximum_fusion), channel_id=1, source_target_pairs={{0,8},{1,9},{2,10},{3,11},{4,12},{5,13},{6,14},{7,15},{8,0},{9,1},... | collective-permute-start | bytes 9437192 | tf_op jit(solution)/shard_map/ppermute | solution.py:20
  32.3 131.8 %copy-start.5 = (bf16[2,64,4096]{2,1,0:T(8,128)(2,1)S(1)}, bf16[2,64,4096]{2,1,0:T(8,128)(2,1)}, u32[]{:S(2)}) copy-start(bf16[2,64,4096]{2,1,0:T(8,128)(2,1)} %copy-done.4) | copy-start | bytes 3145732
  355.3 6.6 %copy-start.8 = (s32[64,2]{0,1:T(2,128)S(1)}, s32[64,2]{0,1:T(2,128)}, u32[]{:S(2)}) copy-start(s32[64,2]{0,1:T(2,128)} %param.15) | copy-start | bytes 1540
  355.3 134.8 %all-to-all-start.1 = ((bf16[16,48,4096]{2,1,0:T(8,128)(2,1)}), bf16[16,48,4096]{2,1,0:T(8,128)(2,1)}, u32[]{:S(2)}, u32[]{:S(2)}) async-start(bf16[16,48,4096]{2,1,0:T(8,128)(2,1)} %bitcast.77), calls=%async_computation.1 | async-start | bytes 12582912 | tf_op jit(solution)/shard_map/all_to_all | solution.py:103
  494.3 9.0 %copy-start.1 = (bf16[64,4096]{1,0:T(8,128)(2,1)S(1)}, bf16[64,4096]{1,0:T(8,128)(2,1)}, u32[]{:S(2)}) copy-start(bf16[64,4096]{1,0:T(8,128)(2,1)} %param.8) | copy-start | bytes 1572868
where the time goes:
time: 513 us; the launch traced here: 503 us
  waiting for transfers between devices  281 us (55%)
  blocking collectives  142 us (28%)
  local copies, waits for them, and re-layouts  29.7 us (6%)
  matrix products  25 us (5%)
  other arithmetic  17.3 us (3%)
  starting transfers between devices  8.14 us (2%)
    ppermute x3, waiting for transfers between devices, shifted(): lax.ppermute(x, axis, [(i, (i + by) % length) for i in range(length)])  153 us
    all_to_all x1, blocking collectives, shards(): lax.all_to_all(copies, 'tile', split_axis=0, concat_axis=0, tiled=True)  142 us
    all_to_all x1, waiting for transfers between devices, shards(): lax.all_to_all(partial_value.reshape(sources, count, D), 'tile', split_ax...  128 us
    unnamed x25, local copies, waits for them, and re-layouts  20.1 us
    dot_general x1, matrix products, expert_apply(): jnp.dot(hidden, second_weight, preferred_element_type=jnp.float32)  13.3 us
  transfers between devices with their start and end apart: 4, of which 4 were waited for; matrix products, arithmetic and copies ran while one was open for 0% of the time, Pallas kernels for 0%

commit v1 on v0

v1 whole, which is shorter than its diff:
```python
import functools
import math

import jax
import jax.numpy as jnp
from jax import lax
from jax.experimental import pallas as pl
from jax.experimental.pallas import tpu as pltpu
from jax.sharding import PartitionSpec as P

HEAD_DIM = 128
D = 4096
SPLIT = 4
TILE_COLS = 8
LANES = 128
SUBLANES = 8

EPSILON = 1e-06
MASKED = -1e30
MESH = pl.DeviceIdType.MESH
VMEM_LIMIT = 60 * 1024 * 1024


def when(cond, body):
    if cond is True:
        body()
    else:
        pl.when(cond)(body)


def both(a, b):
    if a is True:
        return b
    if b is True:
        return a
    return jnp.logical_and(a, b)


def remote(src, dst, send_sem, recv_sem, target):
    return pltpu.make_async_remote_copy(
        src_ref=src,
        dst_ref=dst,
        send_sem=send_sem,
        recv_sem=recv_sem,
        device_id={"tile": target},
        device_id_type=MESH,
    )


def halo_levels(n):
    grid_rows = n // TILE_COLS
    if grid_rows < 2:
        return 1
    return 2 if grid_rows == 2 else 3


def attention_kernel(
    n, rows, q_ref, k_ref, v_ref, mod_ref, att_ref, norm_ref, keys, vals, send_sem, recv_sem, own_sem
):
    me = lax.axis_index("tile")
    grid_rows = n // TILE_COLS
    tile = lax.rem(me + TILE_COLS // 2, n)
    row = lax.div(tile, TILE_COLS)
    col = lax.rem(tile, TILE_COLS)
    if grid_rows < 2:
        verticals = []
    elif grid_rows == 2:
        verticals = [(1, TILE_COLS, True, 1)]
    else:
        verticals = [(1, n - TILE_COLS, row > 0, 2), (2, TILE_COLS, row < grid_rows - 1, 1)]
    sides = [(-1, col > 0), (1, col < TILE_COLS - 1)]
    here = {level: exists for level, _, exists, _ in verticals}
    here[0] = True

    def slot(level, side):
        return level * 3 + 1 + side

    def place(buf, s):
        return buf.at[pl.ds(s * rows, rows), :]

    def over(offset):
        return lax.rem(me + offset + n, n)

    own = [
        pltpu.make_async_copy(src, place(buf, slot(0, 0)), own_sem.at[i])
        for i, (src, buf) in enumerate(((k_ref, keys), (v_ref, vals)))
    ]
    for copy in own:
        copy.start()

    barrier = pltpu.get_barrier_semaphore()
    partners = [(over(offset), exists) for _, offset, exists, _ in verticals]
    partners += [(over(side), exists) for side, exists in sides]
    for target, exists in partners:

        def greet(target=target):
            pl.semaphore_signal(barrier, inc=1, device_id={"tile": target}, device_id_type=MESH)

        when(exists, greet)
    expected = sum(1 if exists is True else jnp.where(exists, 1, 0) for _, exists in partners)
    pl.semaphore_wait(barrier, expected)

    sends = []

    def push(srcs, there, target, exists):
        index = len(sends)
        copies = [
            remote(src, place(buf, there), send_sem.at[index, i], recv_sem.at[there, i], target)
            for i, (src, buf) in enumerate(zip(srcs, (keys, vals)))
        ]

        def go():
            for copy in copies:
                copy.start()

        when(exists, go)
        sends.append((copies, exists))

    def arrived(s, exists):
        def go():
            for i, buf in enumerate((keys, vals)):
                remote(place(buf, s), place(buf, s), send_sem.at[0, i], recv_sem.at[s, i], me).wait_recv()

        when(exists, go)

    for level, offset, exists, there in verticals:
        push((k_ref, v_ref), slot(there, 0), over(offset), exists)
    for side, exists in sides:
        push((k_ref, v_ref), slot(0, -side), over(side), exists)
    for s in range(3 * (1 + len(verticals))):
        level, side = s // 3, s % 3 - 1
        exists = here[level]
        for other, side_exists in sides:
            if other == side:
                exists = both(exists, side_exists)
        if exists is True:
            continue

        def clear(s=s):
            for buf in (keys, vals):
                buf[pl.ds(s * rows, rows), :] = jnp.zeros((rows, D), buf.dtype)

        pl.when(jnp.logical_not(exists))(clear)
    for level, offset, exists, there in verticals:
        arrived(slot(level, 0), exists)
        for side, side_exists in sides:
            push(
                (place(keys, slot(level, 0)), place(vals, slot(level, 0))),
                slot(level, -side),
                over(side),
                both(exists, side_exists),
            )
    for copy in own:
        copy.wait()
    for side, side_exists in sides:
        arrived(slot(0, side), side_exists)
    for level, _, exists, _ in verticals:
        for side, side_exists in sides:
            arrived(slot(level, side), both(exists, side_exists))

    span = 3 * (1 + len(verticals)) * rows
    where = lax.broadcasted_iota(jnp.int32, (rows, span), 1)
    bias = jnp.zeros((rows, span), jnp.float32)
    for s in range(span // rows):
        level, side = s // 3, s % 3 - 1
        exists = here[level]
        for other, side_exists in sides:
            if other == side:
                exists = both(exists, side_exists)
        if exists is True:
            continue
        penalty = jnp.where(exists, 0.0, MASKED)
        bias = jnp.where((where >= s * rows) & (where < (s + 1) * rows), penalty, bias)
    scale = 1.0 / math.sqrt(HEAD_DIM)
    together = 4

    def heads(step, carry):
        for extra in range(together):
            at = pl.ds(pl.multiple_of((step * together + extra) * HEAD_DIM, HEAD_DIM), HEAD_DIM)
            scores = lax.dot_general(
                q_ref[:, at], keys[:, at], (((1,), (1,)), ((), ())), preferred_element_type=jnp.float32
            )
            scores = scores * scale + bias
            raised = jnp.exp(scores - jnp.max(scores, axis=-1, keepdims=True))
            probs = (raised * (1.0 / jnp.sum(raised, axis=-1, keepdims=True))).astype(jnp.bfloat16)
            att_ref[:, at] = jnp.dot(probs, vals[:, at], preferred_element_type=jnp.float32).astype(
                att_ref.dtype
            )
        return carry

    lax.fori_loop(0, D // HEAD_DIM // together, heads, 0)

    def normalise(step, carry):
        at = pl.ds(pl.multiple_of(step * 16, 16), 16)
        wide = att_ref[at, :].astype(jnp.float32)
        wide = wide - jnp.mean(wide, axis=-1, keepdims=True)
        spread = jnp.mean(wide * wide, axis=-1, keepdims=True)
        normed = wide * lax.rsqrt(spread + EPSILON)
        norm_ref[at, :] = (normed * (1.0 + mod_ref[1:2, :]) + mod_ref[0:1, :]).astype(norm_ref.dtype)
        return carry

    lax.fori_loop(0, rows // 16, normalise, 0)
    for copies, exists in sends:

        def drain(copies=copies):
            for copy in copies:
                copy.wait_send()

        when(exists, drain)


def attention(queries, key_rows, values, modulation):
    n = lax.axis_size("tile")
    rows = queries.shape[0]
    levels = halo_levels(n)
    slots = 3 * levels
    vmem = pl.BlockSpec(memory_space=pltpu.VMEM)
    hbm = pl.BlockSpec(memory_space=pl.ANY)
    return pl.pallas_call(
        functools.partial(attention_kernel, n, rows),
        name="halo_attention",
        out_shape=(
            jax.ShapeDtypeStruct((rows, D), jnp.bfloat16),
            jax.ShapeDtypeStruct((rows, D), jnp.bfloat16),
        ),
        in_specs=[vmem, hbm, hbm, vmem],
        out_specs=(vmem, vmem),
        scratch_shapes=[
            pltpu.VMEM((slots * rows, D), jnp.bfloat16),
            pltpu.VMEM((slots * rows, D), jnp.bfloat16),
            pltpu.SemaphoreType.DMA((2 + 3 * (levels - 1), 2)),
            pltpu.SemaphoreType.DMA((slots, 2)),
            pltpu.SemaphoreType.DMA((2,)),
        ],
        compiler_params=pltpu.CompilerParams(
            collective_id=0, has_side_effects=True, vmem_limit_bytes=VMEM_LIMIT
        ),
    )(queries, key_rows, values, modulation)


def plane_order(planes):
    order = [0]
    for step in range(1, planes // 2 + 1):
        for d in (step, planes - step):
            if d not in order:
                order.append(d)
    return order


def expert_kernel(
    n, rows, norm_ref, att_ref, mod_ref, gate_ref, first_ref, second_ref, out_ref,
    tokens, gates, first, second, hidden, part, r1, r2, r3a, r3b, r4,
    send_sem, token_sem, gate_sem, s1_sem, s2_sem, s3a_sem, s3b_sem, s4_sem, own_sem,
):
    planes = n // SPLIT
    half = rows // 2
    width = first_ref.shape[1]
    me = lax.axis_index("tile")
    p = lax.div(me, SPLIT)
    q = lax.rem(me, SPLIT)
    y = lax.div(q, 2)
    c = lax.rem(q, 2)
    order = plane_order(planes)

    def device(plane, yy, cc):
        return plane * SPLIT + yy * 2 + cc

    beside = device(p, 1 - y, c)
    twin = device(p, y, 1 - c)
    plane_of = {d: lax.rem(p + d, planes) for d in order}

    loads = [
        pltpu.make_async_copy(norm_ref, tokens.at[pl.ds(pl.multiple_of(me * rows, rows), rows), :], own_sem.at[0]),
        pltpu.make_async_copy(gate_ref, gates.at[me], own_sem.at[1]),
        pltpu.make_async_copy(first_ref, first, own_sem.at[2]),
        pltpu.make_async_copy(second_ref, second, own_sem.at[3]),
    ]
    for load in loads:
        load.start()

    barrier = pltpu.get_barrier_semaphore()
    for step in range(1, n):
        pl.semaphore_signal(
            barrier, inc=1, device_id={"tile": lax.rem(me + step, n)}, device_id_type=MESH
        )
    pl.semaphore_wait(barrier, n - 1)

    sends = []

    def push(src, dst, recv, target):
        copy = remote(src, dst, send_sem.at[len(sends)], recv, target)
        copy.start()
        sends.append(copy)

    def landed(dst, recv):
        remote(dst, dst, send_sem.at[0], recv, me).wait_recv()

    def block(buf, index, size, offset=0, count=None):
        return buf.at[pl.ds(pl.multiple_of(index * size + offset, half), count or size), :]

    def piece(tile, h):
        return block(tokens, tile, rows, h * half, half)

    def give(tile, h, target):
        push(piece(tile, h), piece(tile, h), token_sem.at[tile, h], target)

    def take(tile, h):
        landed(piece(tile, h), token_sem.at[tile, h])

    loads[0].wait()
    loads[1].wait()
    give(me, 0, beside)
    for d in order[1:]:
        give(me, 1, device(plane_of[d], y, c))
    for h in (0, 1):
        give(me, h, twin)
    give(me, 1, beside)
    for d in order[1:]:
        give(me, 0, device(plane_of[d], y, c))
    for step in range(1, n):
        push(gates.at[me], gates.at[me], gate_sem.at[me], lax.rem(me + step, n))
    take(beside, 0)
    for d in order[1:]:
        give(beside, 0, device(plane_of[d], y, c))
    give(beside, 0, twin)
    take(beside, 1)
    give(beside, 1, twin)

    def forward(d):
        tile = device(plane_of[d], y, c)
        take(tile, 1)
        give(tile, 1, beside)
        give(tile, 1, twin)
        take(tile, 0)
        give(tile, 0, twin)

    def forward_more(d):
        tile = device(plane_of[d], 1 - y, c)
        for h in (0, 1):
            take(tile, h)
            give(tile, h, twin)

    group = SPLIT * rows
    chunk = min(width, 256)
    chunk_out = 512
    eye = lax.broadcasted_iota(jnp.int32, (rows, LANES), 0) == lax.broadcasted_iota(
        jnp.int32, (rows, LANES), 1
    )

    def compute(d):
        plane = plane_of[d]
        for yy in (0, 1):
            for h in (0, 1):
                take(device(plane, yy, 1 - c), h)
        for k in range(SPLIT):
            tile = plane * SPLIT + k
            if d == 0:

                @pl.when(tile != me)
                def _(tile=tile):
                    landed(gates.at[tile], gate_sem.at[tile])
            else:
                landed(gates.at[tile], gate_sem.at[tile])
        at = pl.ds(pl.multiple_of(plane * group, group), group)
        columns = []
        for k in range(SPLIT):
            line = gates[plane * SPLIT + k, pl.ds(p, 1), :]
            columns.append(jnp.sum(jnp.where(eye, line, 0.0), axis=1, keepdims=True))
        weight = jnp.concatenate(columns, axis=0)

        def one(step, carry):
            cols = pl.ds(pl.multiple_of(step * chunk, chunk), chunk)
            raw = jnp.dot(tokens[at, :], first[:, cols], preferred_element_type=jnp.float32)
            hidden[:, cols] = jax.nn.gelu(raw, approximate=True).astype(hidden.dtype)
            return carry

        lax.fori_loop(0, width // chunk, one, 0)

        def two(step, carry):
            cols = pl.ds(pl.multiple_of(step * chunk_out, chunk_out), chunk_out)
            raw = jnp.dot(hidden[...], second[:, cols], preferred_element_type=jnp.float32)
            part[at, cols] = (raw * weight).astype(part.dtype)
            return carry

        lax.fori_loop(0, D // chunk_out, two, 0)
        for yy in (0, 1):
            push(
                block(part, device(plane, yy, 1 - c), rows),
                block(r1, plane * 2 + yy, rows),
                s1_sem.at[plane, yy],
                twin,
            )

    def add(dst, start, terms, count):
        def body(step, carry):
            at = pl.ds(pl.multiple_of(start + step * 16, 16), 16)
            total = dst[at, :].astype(jnp.float32)
            for buf, base in terms:
                total = total + buf[pl.ds(pl.multiple_of(base + step * 16, 16), 16), :].astype(jnp.float32)
            dst[at, :] = total.astype(dst.dtype)
            return carry

        lax.fori_loop(0, count // 16, body, 0)

    def fold_twin(d):
        plane = plane_of[d]
        for yy in (0, 1):
            landed(block(r1, plane * 2 + yy, rows), s1_sem.at[plane, yy])
            add(part, device(plane, yy, c) * rows, [(r1, (plane * 2 + yy) * rows)], rows)
            if d != 0:
                push(
                    block(part, device(plane, yy, c), rows, half, half),
                    block(r3b, p * 2 + yy, half),
                    s3b_sem.at[p, yy],
                    device(plane, y, c),
                )
        push(
            block(part, device(plane, 1 - y, c), rows, 0, half),
            block(r2, plane, half),
            s2_sem.at[plane],
            beside,
        )

    def fold_beside(d):
        plane = plane_of[d]
        landed(block(r2, plane, half), s2_sem.at[plane])
        tile = device(plane, y, c)
        add(part, tile * rows, [(r2, plane * half)], half)
        if d != 0:
            push(
                block(part, tile, rows, 0, half),
                block(r3a, p, half),
                s3a_sem.at[p],
                device(plane, y, c),
            )

    for load in loads[2:]:
        load.wait()
    compute(0)
    for d in order[1:]:
        forward(d)
    for i, d in enumerate(order):
        if i >= 1:
            forward_more(d)
            compute(d)
            fold_twin(order[i - 1])
        if i >= 2:
            fold_beside(order[i - 2])
    fold_twin(order[-1])
    for d in order[-2:]:
        fold_beside(d)

    others = [plane_of[d] for d in order[1:]]
    for source in others:
        landed(block(r3b, source * 2 + 1 - y, half), s3b_sem.at[source, 1 - y])
    add(
        part,
        beside * rows + half,
        [(r3b, (source * 2 + 1 - y) * half) for source in others],
        half,
    )
    push(block(part, beside, rows, half, half), r4, s4_sem, beside)
    for source in others:
        landed(block(r3b, source * 2 + y, half), s3b_sem.at[source, y])
    for source in others:
        landed(block(r3a, source, half), s3a_sem.at[source])
    landed(r4, s4_sem)

    def finish(terms, base):
        def body(step, carry):
            total = None
            for buf, start in terms:
                value = buf[pl.ds(pl.multiple_of(start + step * 16, 16), 16), :].astype(jnp.float32)
                total = value if total is None else total + value
            at = pl.ds(pl.multiple_of(base + step * 16, 16), 16)
            out_ref[at, :] = (att_ref[at, :].astype(jnp.float32) + mod_ref[2:3, :] * total).astype(
                out_ref.dtype
            )
            return carry

        lax.fori_loop(0, half // 16, body, 0)

    finish([(part, me * rows)] + [(r3a, source * half) for source in others], 0)
    finish(
        [(part, me * rows + half), (r4, 0)] + [(r3b, (source * 2 + y) * half) for source in others],
        half,
    )
    for copy in sends:
        copy.wait_send()


def dense_bytes(n, rows, width):
    planes = n // SPLIT
    half = rows // 2
    lines = 2 * n * rows + planes * 2 * rows + 4 * planes * half + half + 3 * rows
    return 2 * (lines * D + 2 * width * D)


def experts_dense(normed, attended, modulation, expert_in, expert_out, routes, gate_fixed):
    n = lax.axis_size("tile")
    rows = normed.shape[0]
    width = expert_in.shape[1]
    planes = n // SPLIT
    half = rows // 2
    lines = -(-planes // SUBLANES) * SUBLANES
    named = routes[None, :, :] == jnp.arange(lines, dtype=jnp.int32)[:, None, None]
    gates = jnp.sum(jnp.where(named, gate_fixed.astype(jnp.float32)[None] / 1024.0, 0.0), axis=2)
    gates = jnp.pad(gates, ((0, 0), (0, LANES - rows)))
    vmem = pl.BlockSpec(memory_space=pltpu.VMEM)
    hbm = pl.BlockSpec(memory_space=pl.ANY)
    dma = pltpu.SemaphoreType.DMA
    count_sends = 5 + 2 * (planes - 1) + (n - 1) + (planes - 1) + 1 + 7 * planes + 2 * planes + 8
    bf = jnp.bfloat16
    return pl.pallas_call(
        functools.partial(expert_kernel, n, rows),
        name="dense_experts",
        out_shape=jax.ShapeDtypeStruct((rows, D), bf),
        in_specs=[hbm, vmem, vmem, hbm, hbm, hbm],
        out_specs=vmem,
        scratch_shapes=[
            pltpu.VMEM((n * rows, D), bf),
            pltpu.VMEM((n, lines, LANES), jnp.float32),
            pltpu.VMEM((D, width), bf),
            pltpu.VMEM((width, D), bf),
            pltpu.VMEM((SPLIT * rows, width), bf),
            pltpu.VMEM((n * rows, D), bf),
            pltpu.VMEM((planes * 2 * rows, D), bf),
            pltpu.VMEM((planes * half, D), bf),
            pltpu.VMEM((planes * half, D), bf),
            pltpu.VMEM((planes * 2 * half, D), bf),
            pltpu.VMEM((half, D), bf),
            dma((count_sends * 2,)),
            dma((n, 2)),
            dma((n,)),
            dma((planes, 2)),
            dma((planes,)),
            dma((planes,)),
            dma((planes, 2)),
            dma(()),
            dma((4,)),
        ],
        compiler_params=pltpu.CompilerParams(
            collective_id=1, has_side_effects=True, vmem_limit_bytes=VMEM_LIMIT
        ),
    )(normed, attended, modulation, gates, expert_in, expert_out)


def slot_table(flat, experts_count):
    onehot = (flat[:, None] == jnp.arange(experts_count, dtype=jnp.int32)[None, :]).astype(
        jnp.int32
    )
    before = jnp.cumsum(onehot, axis=0) - onehot
    return jnp.sum(before * onehot, axis=1)


def expert_apply(rows, first_weight, second_weight):
    hidden = jax.nn.gelu(
        jnp.dot(rows, first_weight, preferred_element_type=jnp.float32), approximate=True
    ).astype(jnp.bfloat16)
    return jnp.dot(hidden, second_weight, preferred_element_type=jnp.float32).astype(jnp.bfloat16)


def experts_sparse(normed, attended, modulation, expert_in, expert_out, routes, gate_fixed):
    devices = lax.axis_size("tile")
    rows_dev = normed.shape[0]
    experts_count = devices // SPLIT
    capacity = 3 * rows_dev // experts_count
    flat = routes.reshape(-1)
    slots = slot_table(flat, experts_count)
    target = flat * capacity + slots
    chooser = (
        target[None, :] == jnp.arange(experts_count * capacity, dtype=jnp.int32)[:, None]
    ).astype(jnp.bfloat16)
    chooser = chooser.reshape(experts_count * capacity, rows_dev, 2).sum(axis=2)
    buffer = jnp.dot(chooser, normed, preferred_element_type=jnp.float32).astype(jnp.bfloat16)
    copies = jnp.broadcast_to(
        buffer.reshape(experts_count, 1, capacity, D), (experts_count, SPLIT, capacity, D)
    ).reshape(devices, capacity, D)
    received = lax.all_to_all(copies, "tile", split_axis=0, concat_axis=0, tiled=True)
    sources = received.shape[0]
    count = received.shape[1]
    partial_value = expert_apply(received.reshape(sources * count, D), expert_in, expert_out)
    returned = lax.all_to_all(
        partial_value.reshape(sources, count, D), "tile", split_axis=0, concat_axis=0, tiled=True
    )
    summed = jnp.sum(
        returned.reshape(experts_count, SPLIT, capacity, D).astype(jnp.float32), axis=1
    )
    expert_rows = summed.astype(jnp.bfloat16).reshape(experts_count * capacity, D)
    picked = jnp.take(expert_rows, target, axis=0).reshape(rows_dev, 2, D)
    gate_scale = gate_fixed.astype(jnp.float32) / 1024.0
    mixture = jnp.sum(picked.astype(jnp.float32) * gate_scale[:, :, None], axis=1)
    return (attended.astype(jnp.float32) + modulation[2] * mixture).astype(jnp.bfloat16)


def shards(queries, key_rows, values, modulation, expert_in, expert_out, routes, gate_fixed):
    attended, normed = attention(queries, key_rows, values, modulation)
    n = lax.axis_size("tile")
    fits = dense_bytes(n, queries.shape[0], expert_in.shape[1]) < VMEM_LIMIT * 3 // 4
    experts = experts_dense if fits else experts_sparse
    return experts(normed, attended, modulation, expert_in, expert_out, routes, gate_fixed)


def solution(mesh):
    placed = (
        P(("groups", "tile"), None),
        P(("groups", "tile"), None),
        P(("groups", "tile"), None),
        P("groups", None),
        P(None, "tile"),
        P("tile", None),
        P(("groups", "tile"), None),
        P(("groups", "tile"), None),
    )
    return jax.shard_map(
        shards, mesh=mesh, in_specs=placed, out_specs=P(("groups", "tile"), None), check_vma=False
    )
```

time: 513 us -> 258 us (0.50); the launches traced: 503 us -> 255 us
  waiting for transfers between devices: 281 us -> 0 us
  Pallas kernels: 0 us -> 251 us
  blocking collectives: 142 us -> 0 us
  local copies, waits for them, and re-layouts: 29.7 us -> 2.47 us
  matrix products: 25 us -> 0 us
  other arithmetic: 17.3 us -> 1.37 us
  starting transfers between devices: 8.14 us -> 0 us
    pallas_call x0 -> x2, Pallas kernels: none -> 251 us  [the longest x1 162 us: experts_dense(): pl.pallas_call(functools.partial(expert_kernel, n, rows), name='dense_exp...]
    ppermute x3 -> x0, waiting for transfers between devices: 153 us -> none  [shifted(): lax.ppermute(x, axis, [(i, (i + by) % length) for i in range(length)])]
    all_to_all x1 -> x0, blocking collectives: 142 us -> none  [shards(): lax.all_to_all(copies, 'tile', split_axis=0, concat_axis=0, tiled=True)]
    all_to_all x1 -> x0, waiting for transfers between devices: 128 us -> none  [shards(): lax.all_to_all(partial_value.reshape(sources, count, D), 'tile', split_ax...]
    dot_general x4 -> x0, matrix products: 25 us -> none  [the longest x1 13.3 us: expert_apply(): jnp.dot(hidden, second_weight, preferred_element_type=jnp.float32)]
    unnamed x25 -> x1, local copies, waits for them, and re-layouts: 20.1 us -> 1.87 us
    reduce_sum x5 -> x1, other arithmetic: 8.81 us -> 0.69 us  [experts_dense(): jnp.sum(jnp.where(named, gate_fixed.astype(jnp.float32)[None] / 1024.0, 0...]
    all_to_all x1 -> x0, starting transfers between devices: 6.23 us -> none  [shards(): lax.all_to_all(partial_value.reshape(sources, count, D), 'tile', split_ax...]
  transfers between devices with their start and end apart: 4 -> 0, of which waited for: 4 -> 0; matrix products, arithmetic and copies ran while one was open for 0% -> 0% of each run, Pallas kernels for 0% -> 0%
where the time goes in v1:
time: 258 us; the launch traced here: 255 us
  Pallas kernels  251 us (97%)
    pallas_call x1, Pallas kernels, experts_dense(): pl.pallas_call(functools.partial(expert_kernel, n, rows), name='dense_exp...  162 us
    pallas_call x1, Pallas kernels, attention(): pl.pallas_call(functools.partial(attention_kernel, n, rows), name='halo_a...  88.8 us

profile of v1, /device:TPU:25, one launch (start us, length us, event | category | flops | bytes accessed | tf_op | source)
XLA Modules:
  0.0 254.9 jit_solution(13772694179931361637)
XLA Ops:
  0.0 0.7 convert_multiply_fusion
  0.7 0.7 select_reduce_fusion
  1.4 0.6 pad.4.gate_ref
  2.0 88.8 %halo_attention.1 = (bf16[64,4096]{1,0:T(8,128)(2,1)}, bf16[64,4096]{1,0:T(8,128)(2,1)}) custom-call(bf16[64,4096]{1,0:T(8,128)(2,1)} %q_ref.1, bf16[64,4096]{1,0:T(8,128)(2,1)} %k_ref.1, bf16[64,4096]{1,0:T(8,128)(2,1)} %v_ref.1, f32[3,4096]{1,0:T(4,128)} %mod_ref.3), custom_call_target="tpu_custom_call" | custom-call | tf_op jit(solution)/shard_map/halo_attention/pallas_call | solution.py:219
  90.7 162.3 %dense_experts.1 = bf16[64,4096]{1,0:T(8,128)(2,1)} custom-call(bf16[64,4096]{1,0:T(8,128)(2,1)} %get-tuple-element.7.norm_ref, bf16[64,4096]{1,0:T(8,128)(2,1)} %get-tuple-element.8.att_ref, f32[3,4096]{1,0:T(4,128)} %mod_ref.3, f32[8,128]{1,0:T(8,128)} %pad.4.gate_ref, bf16[4096,512]{1,0:T(8,128)(2,1)} %first_ref.1, bf16[512,4096]{1,0:T(8,128)(2,1)} %second_ref.1), custom_call_target="tpu_custom_call" | custom-call | tf_op jit(solution)/shard_map/dense_experts/pallas_call | solution.py:514
  253.1 1.9 copy.12

commit v2 on v1

v2 whole, which is shorter than its diff:
```python
import functools
import math

import jax
import jax.numpy as jnp
from jax import lax
from jax.experimental import pallas as pl
from jax.experimental.pallas import tpu as pltpu
from jax.sharding import PartitionSpec as P

HEAD_DIM = 128
D = 4096
SPLIT = 4
TILE_COLS = 8

EPSILON = 1e-06
MASKED = -1e30
MESH = pl.DeviceIdType.MESH
VMEM_LIMIT = 60 * 1024 * 1024


def when(cond, body):
    if cond is True:
        body()
    else:
        pl.when(cond)(body)


def both(a, b):
    if a is True:
        return b
    if b is True:
        return a
    return jnp.logical_and(a, b)


def remote(src, dst, send_sem, recv_sem, target):
    return pltpu.make_async_remote_copy(
        src_ref=src,
        dst_ref=dst,
        send_sem=send_sem,
        recv_sem=recv_sem,
        device_id={"tile": target},
        device_id_type=MESH,
    )


def halo_levels(n):
    grid_rows = n // TILE_COLS
    if grid_rows < 2:
        return 1
    return 2 if grid_rows == 2 else 3


def attention_kernel(
    n, rows, q_ref, k_ref, v_ref, mod_ref, att_ref, norm_ref, keys, vals, send_sem, recv_sem, own_sem
):
    me = lax.axis_index("tile")
    grid_rows = n // TILE_COLS
    tile = lax.rem(me + TILE_COLS // 2, n)
    row = lax.div(tile, TILE_COLS)
    col = lax.rem(tile, TILE_COLS)
    if grid_rows < 2:
        verticals = []
    elif grid_rows == 2:
        verticals = [(1, TILE_COLS, True, 1)]
    else:
        verticals = [(1, n - TILE_COLS, row > 0, 2), (2, TILE_COLS, row < grid_rows - 1, 1)]
    sides = [(-1, col > 0), (1, col < TILE_COLS - 1)]
    here = {level: exists for level, _, exists, _ in verticals}
    here[0] = True

    def slot(level, side):
        return level * 3 + 1 + side

    def place(buf, s):
        return buf.at[pl.ds(s * rows, rows), :]

    def over(offset):
        return lax.rem(me + offset + n, n)

    half = rows // 2
    middle = TILE_COLS // 2
    crossing = {side: col == (middle if side < 0 else middle - 1) for side, _ in sides}
    two = grid_rows == 2

    def part_of(buf, s, h):
        return buf.at[pl.ds(pl.multiple_of(s * rows + h * half, half), half), :]

    own = [
        pltpu.make_async_copy(src, place(buf, slot(0, 0)), own_sem.at[i])
        for i, (src, buf) in enumerate(((k_ref, keys), (v_ref, vals)))
    ]
    for copy in own:
        copy.start()

    def beside(side):
        if not two:
            return over(side)
        return jnp.where(crossing[side], over(side + TILE_COLS), over(side))

    def level_there(level, side):
        return jnp.where(crossing[side], 1 - level, level) if two else level

    barrier = pltpu.get_barrier_semaphore()
    partners = [(over(offset), exists) for _, offset, exists, _ in verticals]
    partners += [(beside(side), exists) for side, exists in sides]
    for target, exists in partners:

        def greet(target=target):
            pl.semaphore_signal(barrier, inc=1, device_id={"tile": target}, device_id_type=MESH)

        when(exists, greet)
    expected = sum(1 if exists is True else jnp.where(exists, 1, 0) for _, exists in partners)
    pl.semaphore_wait(barrier, expected)

    sends = []
    pieces = [(i, h) for i in (0, 1) for h in (0, 1)]
    bufs = (keys, vals)

    def push(i, h, src, there, target, exists):
        copy = remote(
            src,
            part_of(bufs[i], there, h),
            send_sem.at[len(sends)],
            recv_sem.at[there, i * 2 + h],
            target,
        )
        when(exists, copy.start)
        sends.append((copy, exists))

    def arrived(s, exists, i, h):
        ref = part_of(bufs[i], s, h)
        when(exists, remote(ref, ref, send_sem.at[0], recv_sem.at[s, i * 2 + h], me).wait_recv)

    def own_part(i, h):
        return (k_ref, v_ref)[i].at[pl.ds(h * half, half), :]

    for i, h in pieces:
        for level, offset, exists, there in verticals:
            push(i, h, own_part(i, h), slot(there, 0), over(offset), exists)
    for i, h in pieces:
        for side, exists in sides:
            push(i, h, own_part(i, h), slot(level_there(0, side), -side), beside(side), exists)
    for s in range(3 * (1 + len(verticals))):
        level, side = s // 3, s % 3 - 1
        exists = here[level]
        for other, side_exists in sides:
            if other == side:
                exists = both(exists, side_exists)
        if exists is True:
            continue

        def clear(s=s):
            for buf in (keys, vals):
                buf[pl.ds(s * rows, rows), :] = jnp.zeros((rows, D), buf.dtype)

        pl.when(jnp.logical_not(exists))(clear)
    for i, h in pieces:
        for level, offset, exists, there in verticals:
            arrived(slot(level, 0), exists, i, h)
            for side, side_exists in sides:
                push(
                    i,
                    h,
                    part_of(bufs[i], slot(level, 0), h),
                    slot(level_there(level, side), -side),
                    beside(side),
                    both(exists, side_exists),
                )
    for copy in own:
        copy.wait()
    for i, h in pieces:
        for level, exists in sorted(here.items(), key=lambda item: item[0]):
            for side, side_exists in sides:
                arrived(slot(level, side), both(exists, side_exists), i, h)

    span = 3 * (1 + len(verticals)) * rows
    where = lax.broadcasted_iota(jnp.int32, (rows, span), 1)
    bias = jnp.zeros((rows, span), jnp.float32)
    for s in range(span // rows):
        level, side = s // 3, s % 3 - 1
        exists = here[level]
        for other, side_exists in sides:
            if other == side:
                exists = both(exists, side_exists)
        if exists is True:
            continue
        penalty = jnp.where(exists, 0.0, MASKED)
        bias = jnp.where((where >= s * rows) & (where < (s + 1) * rows), penalty, bias)
    scale = 1.0 / math.sqrt(HEAD_DIM)
    together = 4

    def heads(step, carry):
        for extra in range(together):
            at = pl.ds(pl.multiple_of((step * together + extra) * HEAD_DIM, HEAD_DIM), HEAD_DIM)
            scores = lax.dot_general(
                q_ref[:, at], keys[:, at], (((1,), (1,)), ((), ())), preferred_element_type=jnp.float32
            )
            scores = scores * scale + bias
            raised = jnp.exp(scores - jnp.max(scores, axis=-1, keepdims=True))
            probs = (raised * (1.0 / jnp.sum(raised, axis=-1, keepdims=True))).astype(jnp.bfloat16)
            att_ref[:, at] = jnp.dot(probs, vals[:, at], preferred_element_type=jnp.float32).astype(
                att_ref.dtype
            )
        return carry

    lax.fori_loop(0, D // HEAD_DIM // together, heads, 0)

    def normalise(step, carry):
        at = pl.ds(pl.multiple_of(step * 16, 16), 16)
        wide = att_ref[at, :].astype(jnp.float32)
        wide = wide - jnp.mean(wide, axis=-1, keepdims=True)
        spread = jnp.mean(wide * wide, axis=-1, keepdims=True)
        normed = wide * lax.rsqrt(spread + EPSILON)
        norm_ref[at, :] = (normed * (1.0 + mod_ref[1:2, :]) + mod_ref[0:1, :]).astype(norm_ref.dtype)
        return carry

    lax.fori_loop(0, rows // 16, normalise, 0)
    for copy, exists in sends:
        when(exists, copy.wait_send)


def attention(queries, key_rows, values, modulation):
    n = lax.axis_size("tile")
    rows = queries.shape[0]
    levels = halo_levels(n)
    slots = 3 * levels
    vmem = pl.BlockSpec(memory_space=pltpu.VMEM)
    hbm = pl.BlockSpec(memory_space=pl.ANY)
    return pl.pallas_call(
        functools.partial(attention_kernel, n, rows),
        name="halo_attention",
        out_shape=(
            jax.ShapeDtypeStruct((rows, D), jnp.bfloat16),
            jax.ShapeDtypeStruct((rows, D), jnp.bfloat16),
        ),
        in_specs=[vmem, hbm, hbm, vmem],
        out_specs=(vmem, vmem),
        scratch_shapes=[
            pltpu.VMEM((slots * rows, D), jnp.bfloat16),
            pltpu.VMEM((slots * rows, D), jnp.bfloat16),
            pltpu.SemaphoreType.DMA((4 * (2 + 3 * (levels - 1)),)),
            pltpu.SemaphoreType.DMA((slots, 4)),
            pltpu.SemaphoreType.DMA((2,)),
        ],
        compiler_params=pltpu.CompilerParams(
            collective_id=0, has_side_effects=True, vmem_limit_bytes=VMEM_LIMIT
        ),
    )(queries, key_rows, values, modulation)


def nearest_first(p, planes):
    order = [p] + [p * 0] * (planes - 1)
    count = p * 0 + 1
    for step in range(1, planes):
        for other in (p - step, p + step):
            exists = jnp.logical_and(other >= 0, other < planes)
            for i in range(1, planes):
                order[i] = jnp.where(jnp.logical_and(exists, count == i), other, order[i])
            count = count + jnp.where(exists, 1, 0)
    return order


def expert_kernel(
    n, rows, cap, slots_ref, att_ref, mod_ref, high_ref, low_ref, first_ref, second_ref, out_ref,
    tokens, first, second, hidden, part, r1, r2, r3,
    send_sem, token_sem, s1_sem, s2_sem, s3_sem, own_sem,
):
    planes = n // SPLIT
    width = first_ref.shape[1]
    me = lax.axis_index("tile")
    p = lax.div(me, SPLIT)
    q = lax.rem(me, SPLIT)
    y = lax.div(q, 2)
    c = lax.rem(q, 2)
    plane_of = nearest_first(p, planes)

    def device(plane, yy, cc):
        return plane * SPLIT + yy * 2 + cc

    beside = device(p, 1 - y, c)
    twin = device(p, y, 1 - c)

    def block(buf, index):
        return buf.at[pl.ds(pl.multiple_of(index * cap, 16), cap), :]

    loads = [
        pltpu.make_async_copy(block(slots_ref, p), block(tokens, me), own_sem.at[0]),
        pltpu.make_async_copy(first_ref, first, own_sem.at[1]),
        pltpu.make_async_copy(second_ref, second, own_sem.at[2]),
    ]
    for load in loads:
        load.start()

    barrier = pltpu.get_barrier_semaphore()
    targets = [beside, twin] + [device(plane, y, c) for plane in plane_of[1:]]
    for target in targets:
        pl.semaphore_signal(barrier, inc=1, device_id={"tile": target}, device_id_type=MESH)
    pl.semaphore_wait(barrier, len(targets))

    sends = []

    def push(src, dst, recv, target):
        copy = remote(src, dst, send_sem.at[len(sends)], recv, target)
        copy.start()
        sends.append(copy)

    def landed(dst, recv):
        remote(dst, dst, send_sem.at[0], recv, me).wait_recv()

    def give(tile, target):
        push(block(tokens, tile), block(tokens, tile), token_sem.at[tile], target)

    def take(tile):
        landed(block(tokens, tile), token_sem.at[tile])

    for target in (beside, twin):
        push(block(slots_ref, p), block(tokens, me), token_sem.at[me], target)
    for plane in plane_of[1:]:
        push(block(slots_ref, plane), block(tokens, me), token_sem.at[me], device(plane, y, c))

    def forward(i):
        tile = device(plane_of[i], y, c)
        take(tile)
        give(tile, beside)
        give(tile, twin)

    def forward_more(i):
        tile = device(plane_of[i], 1 - y, c)
        take(tile)
        give(tile, twin)

    group = SPLIT * cap
    chunk = min(width, 256)
    chunk_out = 512

    def compute(i):
        plane = plane_of[i]
        for yy in (0, 1):
            take(device(plane, yy, 1 - c))
        at = pl.ds(pl.multiple_of(plane * group, 16), group)

        def one(step, carry):
            cols = pl.ds(pl.multiple_of(step * chunk, chunk), chunk)
            raw = jnp.dot(tokens[at, :], first[:, cols], preferred_element_type=jnp.float32)
            hidden[:, cols] = jax.nn.gelu(raw, approximate=True).astype(hidden.dtype)
            return carry

        lax.fori_loop(0, width // chunk, one, 0)

        def two(step, carry):
            cols = pl.ds(pl.multiple_of(step * chunk_out, chunk_out), chunk_out)
            raw = jnp.dot(hidden[...], second[:, cols], preferred_element_type=jnp.float32)
            part[at, cols] = raw.astype(part.dtype)
            return carry

        lax.fori_loop(0, D // chunk_out, two, 0)
        for yy in (0, 1):
            push(
                block(part, device(plane, yy, 1 - c)),
                block(r1, plane * 2 + yy),
                s1_sem.at[plane, yy],
                twin,
            )

    def add(tile, other, index):
        def body(step, carry):
            at = pl.ds(pl.multiple_of(tile * cap + step * 16, 16), 16)
            extra = other[pl.ds(pl.multiple_of(index * cap + step * 16, 16), 16), :]
            part[at, :] = (part[at, :].astype(jnp.float32) + extra.astype(jnp.float32)).astype(part.dtype)
            return carry

        lax.fori_loop(0, cap // 16, body, 0)

    def fold_twin(i):
        plane = plane_of[i]
        for yy in (1 - y, y):
            landed(block(r1, plane * 2 + yy), s1_sem.at[plane, yy])
            add(device(plane, yy, c), r1, plane * 2 + yy)
            if yy is not y:
                push(block(part, device(plane, yy, c)), block(r2, plane), s2_sem.at[plane], beside)

    def fold_beside(i):
        plane = plane_of[i]
        landed(block(r2, plane), s2_sem.at[plane])
        tile = device(plane, y, c)
        if i == 0:

            def body(step, carry):
                at = pl.ds(pl.multiple_of(p * cap + step * 16, 16), 16)
                mine = part[pl.ds(pl.multiple_of(me * cap + step * 16, 16), 16), :]
                r3[at, :] = (mine.astype(jnp.float32) + r2[at, :].astype(jnp.float32)).astype(r3.dtype)
                return carry

            lax.fori_loop(0, cap // 16, body, 0)
        else:
            add(tile, r2, plane)
            push(block(part, tile), block(r3, p), s3_sem.at[p], tile)

    loads[0].wait()
    take(beside)
    give(beside, twin)
    for load in loads[1:]:
        load.wait()
    if planes > 1:
        forward(1)
    compute(0)
    for i in range(1, planes):
        if i + 1 < planes:
            forward(i + 1)
        forward_more(i)
        compute(i)
        fold_twin(i - 1)
        if i >= 2:
            fold_beside(i - 2)
    fold_twin(planes - 1)
    for i in range(max(planes - 2, 0), planes):
        fold_beside(i)
    for plane in plane_of[1:]:
        landed(block(r3, plane), s3_sem.at[plane])

    def finish(step, carry):
        cols = pl.ds(pl.multiple_of(step * chunk_out, chunk_out), chunk_out)
        found = r3[:, cols]
        mixture = jnp.dot(high_ref[...], found, preferred_element_type=jnp.float32)
        mixture = mixture + jnp.dot(low_ref[...], found, preferred_element_type=jnp.float32)
        out_ref[:, cols] = (
            att_ref[:, cols].astype(jnp.float32) + mod_ref[2:3, cols] * mixture
        ).astype(out_ref.dtype)
        return carry

    lax.fori_loop(0, D // chunk_out, finish, 0)
    for copy in sends:
        copy.wait_send()


def kernel_bytes(n, cap, width):
    planes = n // SPLIT
    lines = 2 * n * cap + planes * 4 * cap
    return 2 * (lines * D + 2 * width * D)


def experts_kernel(normed, attended, modulation, expert_in, expert_out, routes, gate_fixed):
    n = lax.axis_size("tile")
    rows = normed.shape[0]
    width = expert_in.shape[1]
    planes = n // SPLIT
    cap = 3 * rows // planes
    flat = routes.reshape(-1)
    target = flat * cap + slot_table(flat, planes)
    hit = (target[None, :] == jnp.arange(planes * cap, dtype=jnp.int32)[:, None]).astype(jnp.float32)
    chooser = hit.reshape(planes * cap, rows, 2).sum(axis=2).astype(jnp.bfloat16)
    gates = (hit * (gate_fixed.reshape(-1).astype(jnp.float32) / 1024.0)[None, :]).reshape(
        planes * cap, rows, 2
    ).sum(axis=2).T
    coarse = jnp.floor(gates * 128.0) / 128.0
    high = coarse.astype(jnp.bfloat16)
    low = (gates - coarse).astype(jnp.bfloat16)
    slots = jnp.dot(chooser, normed, preferred_element_type=jnp.float32).astype(jnp.bfloat16)
    vmem = pl.BlockSpec(memory_space=pltpu.VMEM)
    hbm = pl.BlockSpec(memory_space=pl.ANY)
    dma = pltpu.SemaphoreType.DMA
    count_sends = 8 * planes + 8
    bf = jnp.bfloat16
    return pl.pallas_call(
        functools.partial(expert_kernel, n, rows, cap),
        name="routed_experts",
        out_shape=jax.ShapeDtypeStruct((rows, D), bf),
        in_specs=[hbm, vmem, vmem, vmem, vmem, hbm, hbm],
        out_specs=vmem,
        scratch_shapes=[
            pltpu.VMEM((n * cap, D), bf),
            pltpu.VMEM((D, width), bf),
            pltpu.VMEM((width, D), bf),
            pltpu.VMEM((SPLIT * cap, width), bf),
            pltpu.VMEM((n * cap, D), bf),
            pltpu.VMEM((planes * 2 * cap, D), bf),
            pltpu.VMEM((planes * cap, D), bf),
            pltpu.VMEM((planes * cap, D), bf),
            dma((count_sends,)),
            dma((n,)),
            dma((planes, 2)),
            dma((planes,)),
            dma((planes,)),
            dma((3,)),
        ],
        compiler_params=pltpu.CompilerParams(
            collective_id=1, has_side_effects=True, vmem_limit_bytes=VMEM_LIMIT
        ),
    )(slots, attended, modulation, high, low, expert_in, expert_out)


def slot_table(flat, experts_count):
    onehot = (flat[:, None] == jnp.arange(experts_count, dtype=jnp.int32)[None, :]).astype(
        jnp.int32
    )
    before = jnp.cumsum(onehot, axis=0) - onehot
    return jnp.sum(before * onehot, axis=1)


def expert_apply(rows, first_weight, second_weight):
    hidden = jax.nn.gelu(
        jnp.dot(rows, first_weight, preferred_element_type=jnp.float32), approximate=True
    ).astype(jnp.bfloat16)
    return jnp.dot(hidden, second_weight, preferred_element_type=jnp.float32).astype(jnp.bfloat16)


def experts_sparse(normed, attended, modulation, expert_in, expert_out, routes, gate_fixed):
    devices = lax.axis_size("tile")
    rows_dev = normed.shape[0]
    experts_count = devices // SPLIT
    capacity = 3 * rows_dev // experts_count
    flat = routes.reshape(-1)
    slots = slot_table(flat, experts_count)
    target = flat * capacity + slots
    chooser = (
        target[None, :] == jnp.arange(experts_count * capacity, dtype=jnp.int32)[:, None]
    ).astype(jnp.bfloat16)
    chooser = chooser.reshape(experts_count * capacity, rows_dev, 2).sum(axis=2)
    buffer = jnp.dot(chooser, normed, preferred_element_type=jnp.float32).astype(jnp.bfloat16)
    copies = jnp.broadcast_to(
        buffer.reshape(experts_count, 1, capacity, D), (experts_count, SPLIT, capacity, D)
    ).reshape(devices, capacity, D)
    received = lax.all_to_all(copies, "tile", split_axis=0, concat_axis=0, tiled=True)
    sources = received.shape[0]
    count = received.shape[1]
    partial_value = expert_apply(received.reshape(sources * count, D), expert_in, expert_out)
    returned = lax.all_to_all(
        partial_value.reshape(sources, count, D), "tile", split_axis=0, concat_axis=0, tiled=True
    )
    summed = jnp.sum(
        returned.reshape(experts_count, SPLIT, capacity, D).astype(jnp.float32), axis=1
    )
    expert_rows = summed.astype(jnp.bfloat16).reshape(experts_count * capacity, D)
    picked = jnp.take(expert_rows, target, axis=0).reshape(rows_dev, 2, D)
    gate_scale = gate_fixed.astype(jnp.float32) / 1024.0
    mixture = jnp.sum(picked.astype(jnp.float32) * gate_scale[:, :, None], axis=1)
    return (attended.astype(jnp.float32) + modulation[2] * mixture).astype(jnp.bfloat16)


def shards(queries, key_rows, values, modulation, expert_in, expert_out, routes, gate_fixed):
    attended, normed = attention(queries, key_rows, values, modulation)
    n = lax.axis_size("tile")
    cap = 3 * queries.shape[0] // (n // SPLIT)
    fits = cap % 16 == 0 and kernel_bytes(n, cap, expert_in.shape[1]) < VMEM_LIMIT * 3 // 4
    experts = experts_kernel if fits else experts_sparse
    return experts(normed, attended, modulation, expert_in, expert_out, routes, gate_fixed)


def solution(mesh):
    placed = (
        P(("groups", "tile"), None),
        P(("groups", "tile"), None),
        P(("groups", "tile"), None),
        P("groups", None),
        P(None, "tile"),
        P("tile", None),
        P(("groups", "tile"), None),
        P(("groups", "tile"), None),
    )
    return jax.shard_map(
        shards, mesh=mesh, in_specs=placed, out_specs=P(("groups", "tile"), None), check_vma=False
    )
```

time: 258 us -> 193 us (0.75)
  the two profiles are of different devices: /device:TPU:25 before, /device:TPU:0 now
where the time goes in v2:
time: 193 us
  Pallas kernels  184 us (95%)
  local copies, waits for them, and re-layouts  2.98 us (2%)
  matrix products  2.79 us (1%)
  other arithmetic  2.54 us (1%)
    pallas_call x1, Pallas kernels, experts_kernel(): pl.pallas_call(functools.partial(expert_kernel, n, rows, cap), name='rout...  115 us
    pallas_call x1, Pallas kernels, attention(): pl.pallas_call(functools.partial(attention_kernel, n, rows), name='halo_a...  69.7 us

profile of v2, /device:TPU:0, one launch (start us, length us, event | category | flops | bytes accessed | tf_op | source)
XLA Modules:
  0.0 192.6 jit_solution(10909584830662408080)
XLA Ops:
  0.0 0.7 convert_multiply_fusion
  0.7 0.8 copy.21
  1.5 0.1 eq.30
  1.6 0.1 fusion.4
  1.7 0.2 reduce_window_sum.11
  1.9 0.2 select_reduce_fusion.1
  2.0 0.1 reduce_sum.30
  2.2 0.1 copy.22
  2.3 0.7 multiply_add_fusion
  3.0 0.1 select_reduce_fusion
  3.1 0.6 fusion.3
  3.7 69.7 %halo_attention.1 = (bf16[64,4096]{1,0:T(8,128)(2,1)}, bf16[64,4096]{1,0:T(8,128)(2,1)}) custom-call(bf16[64,4096]{1,0:T(8,128)(2,1)} %q_ref.1, bf16[64,4096]{1,0:T(8,128)(2,1)} %k_ref.1, bf16[64,4096]{1,0:T(8,128)(2,1)} %v_ref.1, f32[3,4096]{1,0:T(4,128)} %mod_ref.3), custom_call_target="tpu_custom_call" | custom-call | tf_op jit(solution)/shard_map/halo_attention/pallas_call | solution.py:231
  73.4 2.8 %convolution_convert_fusion.slots_ref = bf16[192,4096]{1,0:T(8,128)(2,1)} fusion(bf16[64,4096]{1,0:T(8,128)(2,1)} %get-tuple-element.7, bf16[192,64]{0,1:T(8,128)(2,1)S(1)} %get-tuple-element.10), kind=kOutput, calls=%fused_computation | convolution fusion | flops 101449728 | bytes 2121728 | tf_op jit(solution)/shard_map/dot_general | solution.py:460
  76.2 114.5 %routed_experts.1 = bf16[64,4096]{1,0:T(8,128)(2,1)} custom-call(bf16[192,4096]{1,0:T(8,128)(2,1)} %convolution_convert_fusion.slots_ref, bf16[64,4096]{1,0:T(8,128)(2,1)} %get-tuple-element.8.att_ref, f32[3,4096]{1,0:T(4,128)} %mod_ref.3, bf16[64,192]{1,0:T(8,128)(2,1)} %get-tuple-element.12.high_ref, bf16[64,192]{1,0:T(8,128)(2,1)} %get-tuple-element.11.low_ref, ...), custom_call_target="tpu_custom_call" | custom-call | tf_op jit(solution)/shard_map/routed_experts/pallas_call | solution.py:466
  190.7 1.9 copy.24

commit v3 on v2

--- a/solution.py
+++ b/solution.py
@@ -320,11 +320,22 @@
     for plane in plane_of[1:]:
         push(block(slots_ref, plane), block(tokens, me), token_sem.at[me], device(plane, y, c))
 
-    def forward(i):
+    def forward(i, cond=True, copies=None):
         tile = device(plane_of[i], y, c)
-        take(tile)
-        give(tile, beside)
-        give(tile, twin)
+        if copies is None:
+            copies = []
+            for target in (beside, twin):
+                ref = block(tokens, tile)
+                copies.append(remote(ref, ref, send_sem.at[len(sends)], token_sem.at[tile], target))
+                sends.append(copies[-1])
+
+        def go():
+            take(tile)
+            for copy in copies:
+                copy.start()
+
+        when(cond, go)
+        return copies
 
     def forward_more(i):
         tile = device(plane_of[i], 1 - y, c)
@@ -403,20 +414,23 @@
     give(beside, twin)
     for load in loads[1:]:
         load.wait()
+    inner = jnp.logical_and(p > 0, p < planes - 1)
     if planes > 1:
         forward(1)
+    if planes > 2:
+        early = forward(2, inner)
     compute(0)
+    fold_twin(0)
     for i in range(1, planes):
-        if i + 1 < planes:
+        forward_more(i)
+        if i >= 2 and i + 1 < planes:
             forward(i + 1)
-        forward_more(i)
         compute(i)
-        fold_twin(i - 1)
-        if i >= 2:
-            fold_beside(i - 2)
-    fold_twin(planes - 1)
-    for i in range(max(planes - 2, 0), planes):
-        fold_beside(i)
+        fold_twin(i)
+        fold_beside(i - 1)
+        if i == 1 and planes > 2:
+            forward(2, jnp.logical_not(inner), early)
+    fold_beside(planes - 1)
     for plane in plane_of[1:]:
         landed(block(r3, plane), s3_sem.at[plane])
 

time: 193 us -> 184 us (0.953)
  the two profiles are of different devices: /device:TPU:0 before, /device:TPU:25 now
where the time goes in v3:
time: 184 us; the launch traced here: 183 us
  Pallas kernels  175 us (95%)
  local copies, waits for them, and re-layouts  2.98 us (2%)
  matrix products  2.79 us (2%)
  other arithmetic  2.54 us (1%)
    pallas_call x1, Pallas kernels, experts_kernel(): pl.pallas_call(functools.partial(expert_kernel, n, rows, cap), name='rout...  106 us
    pallas_call x1, Pallas kernels, attention(): pl.pallas_call(functools.partial(attention_kernel, n, rows), name='halo_a...  69.5 us

profile of v3, /device:TPU:25, one launch (start us, length us, event | category | flops | bytes accessed | tf_op | source)
XLA Modules:
  0.0 183.5 jit_solution(9016381366032324043)
XLA Ops:
  0.0 0.7 convert_multiply_fusion
  0.7 0.8 copy.21
  1.5 0.1 eq.30
  1.6 0.1 fusion.4
  1.7 0.2 reduce_window_sum.11
  1.9 0.2 select_reduce_fusion.1
  2.0 0.1 reduce_sum.30
  2.2 0.1 copy.22
  2.3 0.7 multiply_add_fusion
  3.0 0.1 select_reduce_fusion
  3.1 0.6 fusion.3
  3.7 69.5 %halo_attention.1 = (bf16[64,4096]{1,0:T(8,128)(2,1)}, bf16[64,4096]{1,0:T(8,128)(2,1)}) custom-call(bf16[64,4096]{1,0:T(8,128)(2,1)} %q_ref.1, bf16[64,4096]{1,0:T(8,128)(2,1)} %k_ref.1, bf16[64,4096]{1,0:T(8,128)(2,1)} %v_ref.1, f32[3,4096]{1,0:T(4,128)} %mod_ref.3), custom_call_target="tpu_custom_call" | custom-call | tf_op jit(solution)/shard_map/halo_attention/pallas_call | solution.py:231
  73.2 2.8 %convolution_convert_fusion.slots_ref = bf16[192,4096]{1,0:T(8,128)(2,1)} fusion(bf16[64,4096]{1,0:T(8,128)(2,1)} %get-tuple-element.7, bf16[192,64]{0,1:T(8,128)(2,1)S(1)} %get-tuple-element.10), kind=kOutput, calls=%fused_computation | convolution fusion | flops 101449728 | bytes 2121728 | tf_op jit(solution)/shard_map/dot_general | solution.py:474
  76.0 105.6 %routed_experts.1 = bf16[64,4096]{1,0:T(8,128)(2,1)} custom-call(bf16[192,4096]{1,0:T(8,128)(2,1)} %convolution_convert_fusion.slots_ref, bf16[64,4096]{1,0:T(8,128)(2,1)} %get-tuple-element.8.att_ref, f32[3,4096]{1,0:T(4,128)} %mod_ref.3, bf16[64,192]{1,0:T(8,128)(2,1)} %get-tuple-element.12.high_ref, bf16[64,192]{1,0:T(8,128)(2,1)} %get-tuple-element.11.low_ref, ...), custom_call_target="tpu_custom_call" | custom-call | tf_op jit(solution)/shard_map/routed_experts/pallas_call | solution.py:480
  181.6 1.9 %copy.24 = bf16[64,4096]{1,0:T(8,128)(2,1)} copy(bf16[64,4096]{1,0:T(8,128)(2,1)} %routed_experts.1) | data formatting | bytes 1048576

commit v4 on v3

--- a/solution.py
+++ b/solution.py
@@ -53,7 +53,8 @@
 
 
 def attention_kernel(
-    n, rows, q_ref, k_ref, v_ref, mod_ref, att_ref, norm_ref, keys, vals, send_sem, recv_sem, own_sem
+    n, rows, q_ref, k_ref, v_ref, mod_ref, att_ref, norm_ref, keys, vals, send_sem, recv_sem, own_sem,
+    also=None,
 ):
     me = lax.axis_index("tile")
     grid_rows = n // TILE_COLS
@@ -105,6 +106,7 @@
     barrier = pltpu.get_barrier_semaphore()
     partners = [(over(offset), exists) for _, offset, exists, _ in verticals]
     partners += [(beside(side), exists) for side, exists in sides]
+    partners += [(target, True) for target in also or []]
     for target, exists in partners:
 
         def greet(target=target):
@@ -217,6 +219,8 @@
         return carry
 
     lax.fori_loop(0, rows // 16, normalise, 0)
+    if also is not None:
+        return sends
     for copy, exists in sends:
         when(exists, copy.wait_send)
 
@@ -262,42 +266,71 @@
     return order
 
 
-def expert_kernel(
-    n, rows, cap, slots_ref, att_ref, mod_ref, high_ref, low_ref, first_ref, second_ref, out_ref,
+def positions(n):
+    me = lax.axis_index("tile")
+    p = lax.div(me, SPLIT)
+    q = lax.rem(me, SPLIT)
+    return me, p, lax.div(q, 2), lax.rem(q, 2), nearest_first(p, n // SPLIT)
+
+
+def device(plane, yy, cc):
+    return plane * SPLIT + yy * 2 + cc
+
+
+def layer_kernel(
+    n, rows, cap, q_ref, k_ref, v_ref, mod_ref, chooser_ref, high_ref, low_ref, first_ref, second_ref,
+    out_ref, att, norm, slots, keys, vals, halo_send, halo_recv, halo_own,
     tokens, first, second, hidden, part, r1, r2, r3,
     send_sem, token_sem, s1_sem, s2_sem, s3_sem, own_sem,
 ):
-    planes = n // SPLIT
-    width = first_ref.shape[1]
-    me = lax.axis_index("tile")
-    p = lax.div(me, SPLIT)
-    q = lax.rem(me, SPLIT)
-    y = lax.div(q, 2)
-    c = lax.rem(q, 2)
-    plane_of = nearest_first(p, planes)
-
-    def device(plane, yy, cc):
-        return plane * SPLIT + yy * 2 + cc
-
-    beside = device(p, 1 - y, c)
-    twin = device(p, y, 1 - c)
-
-    def block(buf, index):
-        return buf.at[pl.ds(pl.multiple_of(index * cap, 16), cap), :]
-
+    me, p, y, c, plane_of = positions(n)
     loads = [
-        pltpu.make_async_copy(block(slots_ref, p), block(tokens, me), own_sem.at[0]),
         pltpu.make_async_copy(first_ref, first, own_sem.at[1]),
         pltpu.make_async_copy(second_ref, second, own_sem.at[2]),
     ]
     for load in loads:
         load.start()
-
-    barrier = pltpu.get_barrier_semaphore()
-    targets = [beside, twin] + [device(plane, y, c) for plane in plane_of[1:]]
-    for target in targets:
-        pl.semaphore_signal(barrier, inc=1, device_id={"tile": target}, device_id_type=MESH)
-    pl.semaphore_wait(barrier, len(targets))
+    targets = [device(p, 1 - y, c), device(p, y, 1 - c)]
+    targets += [device(plane, y, c) for plane in plane_of[1:]]
+    pending = attention_kernel(
+        n, rows, q_ref, k_ref, v_ref, mod_ref, att, norm, keys, vals, halo_send, halo_recv, halo_own,
+        also=targets,
+    )
+    chunk = 512
+
+    def pick(step, carry):
+        cols = pl.ds(pl.multiple_of(step * chunk, chunk), chunk)
+        slots[:, cols] = jnp.dot(
+            chooser_ref[...], norm[:, cols], preferred_element_type=jnp.float32
+        ).astype(slots.dtype)
+        return carry
+
+    lax.fori_loop(0, D // chunk, pick, 0)
+    expert_part(
+        n, cap, slots, att, mod_ref, high_ref, low_ref, loads, out_ref,
+        tokens, first, second, hidden, part, r1, r2, r3,
+        send_sem, token_sem, s1_sem, s2_sem, s3_sem, own_sem,
+    )
+    for copy, exists in pending:
+        when(exists, copy.wait_send)
+
+
+def expert_part(
+    n, cap, slots_ref, att_ref, mod_ref, high_ref, low_ref, weights, out_ref,
+    tokens, first, second, hidden, part, r1, r2, r3,
+    send_sem, token_sem, s1_sem, s2_sem, s3_sem, own_sem,
+):
+    planes = n // SPLIT
+    width = first.shape[1]
+    me, p, y, c, plane_of = positions(n)
+    beside = device(p, 1 - y, c)
+    twin = device(p, y, 1 - c)
+
+    def block(buf, index):
+        return buf.at[pl.ds(pl.multiple_of(index * cap, 16), cap), :]
+
+    mine = pltpu.make_async_copy(block(slots_ref, p), block(tokens, me), own_sem.at[0])
+    mine.start()
 
     sends = []
 
@@ -400,8 +433,8 @@
 
             def body(step, carry):
                 at = pl.ds(pl.multiple_of(p * cap + step * 16, 16), 16)
-                mine = part[pl.ds(pl.multiple_of(me * cap + step * 16, 16), 16), :]
-                r3[at, :] = (mine.astype(jnp.float32) + r2[at, :].astype(jnp.float32)).astype(r3.dtype)
+                own = part[pl.ds(pl.multiple_of(me * cap + step * 16, 16), 16), :]
+                r3[at, :] = (own.astype(jnp.float32) + r2[at, :].astype(jnp.float32)).astype(r3.dtype)
                 return carry
 
             lax.fori_loop(0, cap // 16, body, 0)
@@ -409,10 +442,10 @@
             add(tile, r2, plane)
             push(block(part, tile), block(r3, p), s3_sem.at[p], tile)
 
-    loads[0].wait()
+    mine.wait()
     take(beside)
     give(beside, twin)
-    for load in loads[1:]:
+    for load in weights:
         load.wait()
     inner = jnp.logical_and(p > 0, p < planes - 1)
     if planes > 1:
@@ -451,13 +484,13 @@
 
 def kernel_bytes(n, cap, width):
     planes = n // SPLIT
-    lines = 2 * n * cap + planes * 4 * cap
+    lines = 2 * n * cap + planes * 5 * cap + 2 * 3 * halo_levels(n) * cap * planes // 3
     return 2 * (lines * D + 2 * width * D)
 
 
-def experts_kernel(normed, attended, modulation, expert_in, expert_out, routes, gate_fixed):
+def layer(queries, key_rows, values, modulation, expert_in, expert_out, routes, gate_fixed):
     n = lax.axis_size("tile")
-    rows = normed.shape[0]
+    rows = queries.shape[0]
     width = expert_in.shape[1]
     planes = n // SPLIT
     cap = 3 * rows // planes
@@ -471,19 +504,28 @@
     coarse = jnp.floor(gates * 128.0) / 128.0
     high = coarse.astype(jnp.bfloat16)
     low = (gates - coarse).astype(jnp.bfloat16)
-    slots = jnp.dot(chooser, normed, preferred_element_type=jnp.float32).astype(jnp.bfloat16)
+    levels = halo_levels(n)
+    tiles = 3 * levels
     vmem = pl.BlockSpec(memory_space=pltpu.VMEM)
     hbm = pl.BlockSpec(memory_space=pl.ANY)
     dma = pltpu.SemaphoreType.DMA
     count_sends = 8 * planes + 8
     bf = jnp.bfloat16
     return pl.pallas_call(
-        functools.partial(expert_kernel, n, rows, cap),
-        name="routed_experts",
+        functools.partial(layer_kernel, n, rows, cap),
+        name="whole_layer",
         out_shape=jax.ShapeDtypeStruct((rows, D), bf),
-        in_specs=[hbm, vmem, vmem, vmem, vmem, hbm, hbm],
+        in_specs=[vmem, hbm, hbm, vmem, vmem, vmem, vmem, hbm, hbm],
         out_specs=vmem,
         scratch_shapes=[
+            pltpu.VMEM((rows, D), bf),
+            pltpu.VMEM((rows, D), bf),
+            pltpu.VMEM((planes * cap, D), bf),
+            pltpu.VMEM((tiles * rows, D), bf),
+            pltpu.VMEM((tiles * rows, D), bf),
+            dma((4 * (2 + 3 * (levels - 1)),)),
+            dma((tiles, 4)),
+            dma((2,)),
             pltpu.VMEM((n * cap, D), bf),
             pltpu.VMEM((D, width), bf),
             pltpu.VMEM((width, D), bf),
@@ -502,7 +544,7 @@
         compiler_params=pltpu.CompilerParams(
             collective_id=1, has_side_effects=True, vmem_limit_bytes=VMEM_LIMIT
         ),
-    )(slots, attended, modulation, high, low, expert_in, expert_out)
+    )(queries, key_rows, values, modulation, chooser, high, low, expert_in, expert_out)
 
 
 def slot_table(flat, experts_count):
@@ -554,12 +596,12 @@
 
 
 def shards(queries, key_rows, values, modulation, expert_in, expert_out, routes, gate_fixed):
-    attended, normed = attention(queries, key_rows, values, modulation)
     n = lax.axis_size("tile")
     cap = 3 * queries.shape[0] // (n // SPLIT)
-    fits = cap % 16 == 0 and kernel_bytes(n, cap, expert_in.shape[1]) < VMEM_LIMIT * 3 // 4
-    experts = experts_kernel if fits else experts_sparse
-    return experts(normed, attended, modulation, expert_in, expert_out, routes, gate_fixed)
+    if cap % 16 == 0 and kernel_bytes(n, cap, expert_in.shape[1]) < VMEM_LIMIT * 3 // 4:
+        return layer(queries, key_rows, values, modulation, expert_in, expert_out, routes, gate_fixed)
+    attended, normed = attention(queries, key_rows, values, modulation)
+    return experts_sparse(normed, attended, modulation, expert_in, expert_out, routes, gate_fixed)
 
 
 def solution(mesh):

time: 184 us -> 180 us (0.978)
  matrix products: 2.79 us -> 0 us
    dot_general x1 -> x0, matrix products: 2.79 us -> none  [experts_kernel(): jnp.dot(chooser, normed, preferred_element_type=jnp.float32)]
    pallas_call x2 -> x1, Pallas kernels: 175 us -> 174 us  [layer(): pl.pallas_call(functools.partial(layer_kernel, n, rows, cap), name='whole...]
where the time goes in v4:
time: 180 us
  Pallas kernels  174 us (97%)
  local copies, waits for them, and re-layouts  3.7 us (2%)
  other arithmetic  2.55 us (1%)
    pallas_call x1, Pallas kernels, layer(): pl.pallas_call(functools.partial(layer_kernel, n, rows, cap), name='whole...  174 us

profile of v4, /device:TPU:25, one launch (start us, length us, event | category | flops | bytes accessed | tf_op | source)
XLA Modules:
  0.0 180.0 jit_solution(17347418016096011926)
XLA Ops:
  0.0 0.7 convert_multiply_fusion
  0.7 0.8 copy.22
  1.5 0.1 eq.30
  1.6 0.1 fusion.4
  1.7 0.2 reduce_window_sum.11
  1.9 0.2 select_reduce_fusion.1
  2.0 0.1 reduce_sum.30
  2.2 0.1 copy.23
  2.3 0.7 multiply_add_fusion
  3.0 0.1 select_reduce_fusion
  3.1 0.6 fusion.3
  3.7 0.7 copy.24.chooser_ref
  4.4 173.7 %whole_layer.1 = bf16[64,4096]{1,0:T(8,128)(2,1)} custom-call(bf16[64,4096]{1,0:T(8,128)(2,1)} %q_ref.1, bf16[64,4096]{1,0:T(8,128)(2,1)} %k_ref.1, bf16[64,4096]{1,0:T(8,128)(2,1)} %v_ref.1, f32[3,4096]{1,0:T(4,128)} %mod_ref.1, bf16[192,64]{1,0:T(8,128)(2,1)} %copy.24.chooser_ref, bf16[64,192]{1,0:T(8,128)(2,1)} %get-tuple-element.8.high_ref, ...), custom_call_target="tpu_custom_call" | custom-call | tf_op jit(solution)/shard_map/whole_layer/pallas_call | solution.py:514
  178.1 1.9 %copy.26 = bf16[64,4096]{1,0:T(8,128)(2,1)} copy(bf16[64,4096]{1,0:T(8,128)(2,1)} %whole_layer.1) | data formatting | bytes 1048576

commit v5 on v4

--- a/solution.py
+++ b/solution.py
@@ -191,7 +191,7 @@
         penalty = jnp.where(exists, 0.0, MASKED)
         bias = jnp.where((where >= s * rows) & (where < (s + 1) * rows), penalty, bias)
     scale = 1.0 / math.sqrt(HEAD_DIM)
-    together = 4
+    together = 8
 
     def heads(step, carry):
         for extra in range(together):
@@ -496,11 +496,15 @@
     cap = 3 * rows // planes
     flat = routes.reshape(-1)
     target = flat * cap + slot_table(flat, planes)
-    hit = (target[None, :] == jnp.arange(planes * cap, dtype=jnp.int32)[:, None]).astype(jnp.float32)
-    chooser = hit.reshape(planes * cap, rows, 2).sum(axis=2).astype(jnp.bfloat16)
-    gates = (hit * (gate_fixed.reshape(-1).astype(jnp.float32) / 1024.0)[None, :]).reshape(
-        planes * cap, rows, 2
-    ).sum(axis=2).T
+    target = target.reshape(rows, 2)
+    scale = gate_fixed.astype(jnp.float32) / 1024.0
+    lines = jnp.arange(planes * cap, dtype=jnp.int32)
+    chooser = sum(
+        (target[None, :, k] == lines[:, None]).astype(jnp.float32) for k in range(2)
+    ).astype(jnp.bfloat16)
+    gates = sum(
+        jnp.where(target[:, k, None] == lines[None, :], scale[:, k, None], 0.0) for k in range(2)
+    )
     coarse = jnp.floor(gates * 128.0) / 128.0
     high = coarse.astype(jnp.bfloat16)
     low = (gates - coarse).astype(jnp.bfloat16)

time: 180 us -> 179 us (level)
  Pallas kernels: 174 us -> 172 us
where the time goes in v5:
time: 179 us; the launch traced here: 178 us
  Pallas kernels  172 us (96%)
  other arithmetic  3.19 us (2%)
  local copies, waits for them, and re-layouts  3 us (2%)
    pallas_call x1, Pallas kernels, layer(): pl.pallas_call(functools.partial(layer_kernel, n, rows, cap), name='whole...  172 us

profile of v5, /device:TPU:25, one launch (start us, length us, event | category | flops | bytes accessed | tf_op | source)
XLA Modules:
  0.0 178.5 jit_solution(17337482003325182866)
XLA Ops:
  0.0 0.7 convert_multiply_fusion
  0.7 0.8 copy.15
  1.5 0.1 eq.71
  1.6 0.1 fusion.1
  1.7 0.2 reduce_window_sum.11
  1.9 0.2 select_reduce_fusion
  2.0 0.1 reduce_sum.12
  2.2 0.1 copy.16
  2.3 0.7 multiply_add_fusion
  3.0 0.6 add_convert_fusion.chooser_ref
  3.6 0.7 subtract_convert_fusion
  4.3 172.3 %whole_layer.1 = bf16[64,4096]{1,0:T(8,128)(2,1)} custom-call(bf16[64,4096]{1,0:T(8,128)(2,1)} %q_ref.1, bf16[64,4096]{1,0:T(8,128)(2,1)} %k_ref.1, bf16[64,4096]{1,0:T(8,128)(2,1)} %v_ref.1, f32[3,4096]{1,0:T(4,128)} %mod_ref.1, bf16[192,64]{1,0:T(8,128)(2,1)} %add_convert_fusion.chooser_ref, bf16[64,192]{1,0:T(8,128)(2,1)} %get-tuple-element.6.high_ref, ...), custom_call_target="tpu_custom_call" | custom-call | tf_op jit(solution)/shard_map/whole_layer/pallas_call | solution.py:518
  176.6 1.9 %copy.18 = bf16[64,4096]{1,0:T(8,128)(2,1)} copy(bf16[64,4096]{1,0:T(8,128)(2,1)} %whole_layer.1) | data formatting | bytes 1048576
  (2 shorter events, 0.0 us)
